TPU v7x, 128 devices: a whole 4x4x4 slice. The times are simulated.
128 devices in a mesh: patch: 8 (over x, core), proto: 16 (over z, y).
Axes of the slice: x: 4, y: 4, z: 4, core: 2. Of those that a mesh axis runs over, the one named last changes fastest.
Arguments:
- student_feats: bfloat16 [32768, 256], P(('patch', 'proto')), may hold values from -50 to 50
- teacher_feats: bfloat16 [32768, 256], P(('patch', 'proto')), may hold values from -50 to 50
- proto_weight: bfloat16 [256, 131072], P(None, 'proto'), may hold values from -4 to 4
- mask_index: int32 [4096], P(('patch', 'proto')), may hold values from 0 to 255, as said below
- row_weight: bfloat16 [4096], P(('patch', 'proto')), may hold values from 0.5 to 4
Outputs:
- grad_student: float32 [4096, 256], P(('patch', 'proto'))
- grad_proto: float32 [256, 131072], P('patch', 'proto')
- loss: float32 [], replicated
Inputs may be any that keep to these rules, and one draw needn't show every extreme that they name: `mask_index`: entries k * 32 to (k + 1) * 32 - 1 are distinct patch positions of image k, counted from that image's first patch.
All inputs are finite; a program needn't handle non-finite values.
Results may differ from a plain program's by a relative error of at most 0.0057.
Values may be sent and summed in bfloat16 or wider, within the bound.
No kernel may reach another device: no remote copies, remote signals or barrier semaphores. Data moves between devices by JAX's collectives and lax.ppermute only.
A program may use at most 128 MiB of HBM per device.

v0:
```python
import jax
import jax.numpy as jnp
from jax import lax
from jax.sharding import PartitionSpec as P

SK_ITERS = 3
eps = 1e-06
teacher_temp = 0.07
student_temp = 0.1


def unit_rows(values):
    values = values.astype(jnp.float32)
    inverse = lax.rsqrt(jnp.sum(values * values, axis=1) + eps)
    return (values * inverse[:, None], inverse)


def finish(teacher_exp, scale_rows, scale_cols, logits, exp_logits, exp_total, weights):
    codes = teacher_exp * scale_rows[:, None] * scale_cols[None, :]
    student_probs = exp_logits / exp_total[:, None]
    grad_logits = (weights[:, None] * (student_probs - codes)).astype(jnp.bfloat16)
    log_total = jnp.log(exp_total)
    loss_partial = jnp.sum(weights[:, None] * codes * (log_total[:, None] - logits))
    return (grad_logits, loss_partial)


def feature_term(grad_logits, proto_cols):
    return (
        lax.dot_general(
            grad_logits, proto_cols, (((1,), (1,)), ((), ())), preferred_element_type=jnp.float32
        )
        / student_temp
    )


def head_term(student_rows, grad_logits):
    return (
        lax.dot_general(
            student_rows, grad_logits, (((0,), (0,)), ((), ())), preferred_element_type=jnp.float32
        )
        / student_temp
    )


def on_device(student_feats, teacher_feats, proto_weight, mask_index, row_weight):
    highest = lax.Precision.HIGHEST
    unit_student, inverse_student = unit_rows(jnp.take(student_feats, mask_index, axis=0))
    unit_teacher, _ = unit_rows(jnp.take(teacher_feats, mask_index, axis=0))
    own_student = unit_student.astype(jnp.bfloat16)
    own_teacher = unit_teacher.astype(jnp.bfloat16)
    w_float = proto_weight.astype(jnp.float32)
    col_inverse = lax.rsqrt(jnp.sum(w_float * w_float, axis=0) + eps)
    unit_proto = w_float * col_inverse[None, :]
    proto_unit = unit_proto.astype(jnp.bfloat16)
    teacher_rows, student_rows, weights = (
        lax.all_gather(own_teacher, "proto", axis=0, tiled=True),
        lax.all_gather(own_student, "proto", axis=0, tiled=True),
        lax.all_gather(row_weight, "proto", axis=0, tiled=True),
    )
    weights = weights.astype(jnp.float32)
    teacher_exp = jnp.exp(
        jnp.dot(teacher_rows, proto_unit, preferred_element_type=jnp.float32) / teacher_temp
    )
    scale_rows = jnp.ones((teacher_rows.shape[0],), jnp.float32)
    for sweep in range(SK_ITERS):
        col_part = jnp.dot(scale_rows, teacher_exp, precision=highest)
        scale_cols = 1.0 / lax.psum(col_part, "patch")
        row_part = jnp.dot(teacher_exp, scale_cols, precision=highest)
        scale_rows = 1.0 / lax.psum(row_part, "proto")
    logits = jnp.dot(student_rows, proto_unit, preferred_element_type=jnp.float32) / student_temp
    exp_logits = jnp.exp(logits)
    exp_total = lax.psum(jnp.sum(exp_logits, axis=1), "proto")
    grad_logits, loss_partial = finish(
        teacher_exp, scale_rows, scale_cols, logits, exp_logits, exp_total, weights
    )
    feature_grad = lax.psum_scatter(
        feature_term(grad_logits, proto_unit), "proto", scatter_dimension=0, tiled=True
    )
    row_share = proto_unit.shape[0] // lax.axis_size("patch")
    row_offset = lax.axis_index("patch") * row_share
    head_full = lax.psum(head_term(student_rows, grad_logits), "patch")
    inner = jnp.sum(unit_proto * head_full, axis=0)
    whole_grad = col_inverse[None, :] * (head_full - unit_proto * inner[None, :])
    grad_proto = lax.dynamic_slice_in_dim(whole_grad, row_offset, row_share, 0)
    loss_total, weight_total = lax.psum(
        (loss_partial, jnp.sum(row_weight.astype(jnp.float32))), ("patch", "proto")
    )
    grad_student = inverse_student[:, None] * (
        feature_grad - unit_student * jnp.sum(unit_student * feature_grad, axis=1)[:, None]
    )
    return (grad_student, grad_proto, loss_total / weight_total)


def solution(mesh):
    in_specs = (
        P(("patch", "proto"), None),
        P(("patch", "proto"), None),
        P(None, "proto"),
        P(("patch", "proto")),
        P(("patch", "proto")),
    )
    out_specs = (P(("patch", "proto"), None), P("patch", "proto"), P())
    return jax.shard_map(
        on_device, mesh=mesh, in_specs=in_specs, out_specs=out_specs, check_vma=False
    )
```

profile of v0, /device:TPU:1, one launch (start us, length us, event | category | flops | bytes accessed | tf_op | source)
XLA Modules:
  0.0 526.8 jit_solution(3142531026962949100)
XLA Ops:
  8.1 0.7 compare_select_fusion
  8.7 0.7 compare_and_fusion
  9.4 0.6 gather_fusion
  10.1 1.5 gather_fusion.1
  11.9 20.8 %all_gather.11 = bf16[512,256]{1,0:T(8,128)(2,1)S(1)} all-gather(bf16[32,256]{1,0:T(8,128)(2,1)S(1)} %get-tuple-element.15), channel_id=1, replica_groups=mesh['patch'=8,'proto'=16] {'proto'}, dimensions={0}, use_global_device_ids=true | all-gather | bytes 278528 | tf_op jit(solution)/shard_map/all_gather | solution.py:56
  32.7 3.1 fusion
  35.8 4.5 multiply_exponential_fusion
  40.3 7.9 %fusion.20 = f32[1,8192]{1,0:T(1,128)S(1)} fusion(f32[512,8192]{1,0:T(8,128)S(1)} %multiply_exponential_fusion), kind=kOutput, calls=%fused_computation.41 | convolution fusion | flops 50331648 | bytes 16809984 | tf_op jit(solution)/shard_map/dot_general | solution.py:66
  48.2 26.1 %psum.71 = f32[8192]{0:T(1024)S(1)} all-reduce(f32[8192]{0:T(1024)S(1)} %bitcast.33), channel_id=1, replica_groups=mesh['patch'=8,'proto'=16] {'patch'}, use_global_device_ids=true, to_apply=%region_5.7 | all-reduce | flops 8192 | bytes 65536 | tf_op jit(solution)/shard_map/psum | solution.py:67
  74.4 17.6 %fusion.23 = f32[1,512]{1,0:T(1,128)S(1)} fusion(f32[512,8192]{1,0:T(8,128)} %copy-done.2, f32[8192,1]{0,1:T(1,128)S(1)} %bitcast.29), kind=kOutput, calls=%fused_computation.50 | convolution fusion | flops 50331648 | bytes 16812032 | tf_op jit(solution)/shard_map/dot_general | solution.py:68
  92.0 31.0 %psum.72 = f32[512]{0:T(512)S(1)} all-reduce(f32[512]{0:T(512)S(1)} %bitcast.35), channel_id=1, replica_groups=mesh['patch'=8,'proto'=16] {'proto'}, use_global_device_ids=true, to_apply=%region_6.8 | all-reduce | flops 512 | bytes 4096 | tf_op jit(solution)/shard_map/psum | solution.py:69
  123.0 11.5 %fusion.24 = f32[1,8192]{1,0:T(1,128)S(1)} fusion(f32[512,1]{0,1:T(1,128)S(1)} %bitcast.37, f32[512,8192]{1,0:T(8,128)} %copy-done.2), kind=kOutput, calls=%fused_computation.51 | convolution fusion | flops 50331648 | bytes 16812032 | tf_op jit(solution)/shard_map/dot_general | solution.py:66
  134.5 30.9 %psum.73 = f32[8192]{0:T(1024)S(1)} all-reduce(f32[8192]{0:T(1024)S(1)} %bitcast.30), channel_id=1, replica_groups=mesh['patch'=8,'proto'=16] {'patch'}, use_global_device_ids=true, to_apply=%region_7.9 | all-reduce | flops 8192 | bytes 65536 | tf_op jit(solution)/shard_map/psum | solution.py:67
  165.4 17.6 %fusion.25 = f32[1,512]{1,0:T(1,128)S(1)} fusion(f32[512,8192]{1,0:T(8,128)} %copy-done.2, f32[8192,1]{0,1:T(1,128)S(1)} %bitcast.31), kind=kOutput, calls=%fused_computation.52 | convolution fusion | flops 50331648 | bytes 16812032 | tf_op jit(solution)/shard_map/dot_general | solution.py:68
  183.0 28.5 %psum.74 = f32[512]{0:T(512)S(1)} all-reduce(f32[512]{0:T(512)S(1)} %bitcast.36), channel_id=1, replica_groups=mesh['patch'=8,'proto'=16] {'proto'}, use_global_device_ids=true, to_apply=%region_8.10 | all-reduce | flops 512 | bytes 4096 | tf_op jit(solution)/shard_map/psum | solution.py:69
  211.5 11.5 %fusion.26 = f32[1,8192]{1,0:T(1,128)S(1)} fusion(f32[512,1]{0,1:T(1,128)S(1)} %bitcast.38, f32[512,8192]{1,0:T(8,128)} %copy-done.2), kind=kOutput, calls=%fused_computation.53 | convolution fusion | flops 50331648 | bytes 16812032 | tf_op jit(solution)/shard_map/dot_general | solution.py:66
  223.0 31.0 %psum.75 = f32[8192]{0:T(1024)S(1)} all-reduce(f32[8192]{0:T(1024)S(1)} %bitcast.32), channel_id=1, replica_groups=mesh['patch'=8,'proto'=16] {'patch'}, use_global_device_ids=true, to_apply=%region_9.11 | all-reduce | flops 8192 | bytes 65536 | tf_op jit(solution)/shard_map/psum | solution.py:67
  254.0 17.8 %fusion.27 = f32[1,512]{1,0:T(1,128)S(1)} fusion(f32[512,8192]{1,0:T(8,128)} %copy-done.2, f32[8192,1]{0,1:T(1,128)S(1)} %bitcast.28), kind=kOutput, calls=%fused_computation.54 | convolution fusion | flops 50331648 | bytes 16812032 | tf_op jit(solution)/shard_map/dot_general | solution.py:68
  271.7 17.8 %all_gather.10 = bf16[512,256]{1,0:T(8,128)(2,1)S(1)} all-gather(bf16[32,256]{1,0:T(8,128)(2,1)S(1)} %get-tuple-element.14), channel_id=1, replica_groups=mesh['patch'=8,'proto'=16] {'proto'}, dimensions={0}, use_global_device_ids=true | all-gather | bytes 278528 | tf_op jit(solution)/shard_map/all_gather | solution.py:57
  289.5 7.5 %exponential_reduce_fusion = (f32[512]{0:T(512)S(1)}, f32[512,8192]{1,0:T(8,128)}) fusion(bf16[512,256]{1,0:T(8,128)(2,1)S(1)} %all_gather.10, f32[8192]{0:T(1024)S(1)} %add_rsqrt_fusion, bf16[256,8192]{1,0:T(8,128)(2,1)S(1)} %copy-done.3), kind=kOutput, calls=%fused_computation.6 | convolution fusion | flops 2162163200 | bytes 21268480 | tf_op jit(solution)/shard_map/dot_general | solution.py:70
  297.0 30.9 %all-reduce.2 = (f32[512]{0:T(512)S(1)}, f32[512]{0:T(512)S(1)}) all-reduce(f32[512]{0:T(512)S(1)} %bitcast.34, f32[512]{0:T(512)S(1)} %get-tuple-element.16), channel_id=1, replica_groups=mesh['patch'=8,'proto'=16] {'proto'}, use_global_device_ids=true, to_apply=%region_10.12 | all-reduce | flops 1024 | bytes 8192 | tf_op jit(solution)/shard_map/psum | solution.py:69
  329.4 29.0 %all-reduce = bf16[512]{0:T(512)(128)(2,1)S(1)} all-reduce(bf16[512]{0:T(512)(128)(2,1)S(1)} %dynamic-update-slice), channel_id=1, replica_groups=mesh['patch'=8,'proto'=16] {'proto'}, use_global_device_ids=true, to_apply=%add | all-reduce | flops 512 | bytes 2048
  358.4 14.4 %multiply_reduce_fusion = (f32[]{:T(128)}, bf16[512,8192]{1,0:T(8,128)(2,1)S(1)}) fusion(f32[512,8192]{1,0:T(8,128)} %copy-done.2, f32[512,8192]{1,0:T(8,128)} %get-tuple-element.17, f32[512]{0:T(512)S(1)} %log.3, f32[8192]{0:T(1024)S(1)} %broadcast_divide_fusion, f32[512]{0:T(512)S(1)} %broadcast_divide_fusion.5, f32[512]{0:T(512)S(1)} %convert_element_type.28, ...), kind=kLoop, calls=%fused_computation.2 | loop fusion | flops 46137344 | bytes 41984004 | tf_op jit(solution)/shard_map/reduce_sum | solution.py:23
  372.9 3.2 copy-done.5
  376.1 3.2 fusion.7
  379.4 9.0 %convolution_multiply_fusion = f32[256,8192]{1,0:T(8,128)} fusion(bf16[512,256]{1,0:T(8,128)(2,1)S(1)} %all_gather.10, bf16[512,8192]{1,0:T(8,128)(2,1)} %copy-done.5), kind=kOutput, calls=%fused_computation.7 | convolution fusion | flops 2149580800 | bytes 17039360 | tf_op jit(solution)/shard_map/dot_general | solution.py:38
  389.0 85.0 %all-reduce.1 = (f32[]{:T(128)}, f32[]{:T(128)}) all-reduce(f32[]{:T(128)} %get-tuple-element.10, f32[]{:T(128)} %convert_reduce_fusion), channel_id=1, replica_groups=mesh['patch'=8,'proto'=16] {'patch','proto'}, use_global_device_ids=true, to_apply=%region_16.18 | all-reduce | flops 2 | bytes 16 | tf_op jit(solution)/shard_map/psum | solution.py:85
  475.3 0.9 fusion.14
  476.3 1.5 fusion.16
  477.8 32.0 %all-reduce.5.cloned.1.call-done = f32[256,8192]{1,0:T(8,128)} async-done(((f32[256,8192]{1,0:T(8,128)}), f32[256,8192]{1,0:T(8,128)}) %all-reduce.5.cloned.1.call-update) | async-done | bytes 8388624 | tf_op jit(solution)/shard_map/psum | solution.py:81
  509.8 6.0 %multiply_reduce_fusion.1 = (f32[8192]{0:T(1024)S(1)}, f32[256,8192]{1,0:T(8,128)S(1)}) fusion(f32[256,8192]{1,0:T(8,128)} %all-reduce.5.cloned.1.call-done, f32[8192]{0:T(1024)S(1)} %add_rsqrt_fusion, bf16[256,8192]{1,0:T(8,128)(2,1)} %param.9), kind=kLoop, calls=%fused_computation.11 | loop fusion | flops 8380416 | bytes 21037056 | tf_op jit(solution)/shard_map/reduce_sum | solution.py:82
  515.7 2.3 fusion.10
  (37 shorter events, 2.0 us)
Async XLA Ops:
  8.0 1.4 copy-start
  8.0 467.3 %reduce-scatter.2.cloned.1.call-start = ((), (), s32[]{:S(2)}) async-start(), calls=%async_computation.1 | async-start | bytes 557056 | tf_op jit(solution)/shard_map/reduce_scatter | solution.py:76
  40.3 8.0 %copy-start.2 = (f32[512,8192]{1,0:T(8,128)}, f32[512,8192]{1,0:T(8,128)S(1)}, u32[]{:S(2)}) copy-start(f32[512,8192]{1,0:T(8,128)S(1)} %multiply_exponential_fusion) | copy-start | bytes 50331652
  253.9 35.6 %copy-start.3 = (bf16[256,8192]{1,0:T(8,128)(2,1)S(1)}, bf16[256,8192]{1,0:T(8,128)(2,1)}, u32[]{:S(2)}) copy-start(bf16[256,8192]{1,0:T(8,128)(2,1)} %param.9) | copy-start | bytes 12582916
  289.5 38.4 %copy-start.7 = (u32[128]{0:T(128)S(1)}, u32[128]{0:T(128)}, u32[]{:S(2)}) copy-start(u32[128]{0:T(128)} %constant.44) | copy-start | bytes 1540
  289.5 39.6 %copy-start.6 = (bf16[32]{0:T(256)(128)(2,1)S(1)}, bf16[32]{0:T(256)(128)(2,1)}, u32[]{:S(2)}) copy-start(bf16[32]{0:T(256)(128)(2,1)} %param.11) | copy-start | bytes 196
  358.4 17.7 %copy-start.4 = (bf16[256,8192]{1,0:T(8,128)(2,1)S(1)}, bf16[256,8192]{1,0:T(8,128)(2,1)}, u32[]{:S(2)}) copy-start(bf16[256,8192]{1,0:T(8,128)(2,1)} %param.9) | copy-start | bytes 12582916
  372.9 3.2 copy-start.5
  379.3 130.5 %all-reduce.5.cloned.1.call-start = ((), (), s32[]{:S(2)}) async-start(), calls=%async_computation.2 | async-start | bytes 16777216 | tf_op jit(solution)/shard_map/psum | solution.py:81
  476.2 41.8 %copy-start.1 = (bf16[256,256]{1,0:T(8,128)(2,1)S(1)}, bf16[256,256]{1,0:T(8,128)(2,1)}, u32[]{:S(2)}) copy-start(bf16[256,256]{1,0:T(8,128)(2,1)} %param.7) | copy-start | bytes 393220
Sparse Core Ops, SparseCore 0:
  379.4 87.7 reduce-scatter.1
Sparse Core Ops, SparseCore 1:
  388.5 121.3 all-reduce.4
where the time goes:
time: 536 us; the launch traced here: 527 us
  blocking collectives  331 us (62%)
  matrix products  108 us (20%)
  waiting for transfers between devices  32.1 us (6%)
  other arithmetic  30.5 us (6%)
  between operations  18.9 us (4%)
  local copies, waits for them, and re-layouts  6.24 us (1%)
    psum x3, blocking collectives, on_device(): scale_rows = 1.0 / lax.psum(row_part, 'proto')  90.4 us
    psum x3, blocking collectives, on_device(): scale_cols = 1.0 / lax.psum(col_part, 'patch')  88 us
    psum x1, blocking collectives, on_device(): lax.psum((loss_partial, jnp.sum(row_weight.astype(jnp.float32))), ('patch...  85 us
    dot_general x3, matrix products, on_device(): row_part = jnp.dot(teacher_exp, scale_cols, precision=highest)  53 us
    psum x1, waiting for transfers between devices, on_device(): head_full = lax.psum(head_term(student_rows, grad_logits), 'patch')  32 us
    dot_general x3, matrix products, on_device(): col_part = jnp.dot(scale_rows, teacher_exp, precision=highest)  30.8 us
    unnamed x1, blocking collectives  29 us
    all_gather x1, blocking collectives, on_device(): lax.all_gather(own_teacher, 'proto', axis=0, tiled=True)  20.8 us
  transfers between devices with their start and end apart: 2, of which 1 were waited for; matrix products, arithmetic and copies ran while one was open for 2% of the time, Pallas kernels for 0%

commit v1 on v0

--- a/solution.py
+++ b/solution.py
@@ -53,7 +53,9 @@
     unit_proto = w_float * col_inverse[None, :]
     proto_unit = unit_proto.astype(jnp.bfloat16)
     teacher_rows, student_rows, weights = (
-        lax.all_gather(own_teacher, "proto", axis=0, tiled=True),
+        jnp.concatenate(
+            lax.all_to_all(jnp.stack([own_teacher] * lax.axis_size("proto")), "proto", 0, 0), axis=0
+        ),
         lax.all_gather(own_student, "proto", axis=0, tiled=True),
         lax.all_gather(row_weight, "proto", axis=0, tiled=True),
     )

time: 536 us -> 518 us (0.966)
  blocking collectives: 331 us -> 306 us
  starting transfers between devices: 0.08 us -> 9.15 us
    all_gather x1 -> x0, blocking collectives: 20.8 us -> none  [on_device(): lax.all_gather(own_teacher, 'proto', axis=0, tiled=True)]
    psum x1, blocking collectives: 85 us -> 73.2 us  [on_device(): lax.psum((loss_partial, jnp.sum(row_weight.astype(jnp.float32))), ('patch...]
    all_to_all x0 -> x1, starting transfers between devices: none -> 8.6 us  [on_device(): lax.all_to_all(jnp.stack([own_teacher] * lax.axis_size('proto')), 'proto'...]
    psum x3, blocking collectives: 88 us -> 95.6 us  [on_device(): scale_cols = 1.0 / lax.psum(col_part, 'patch')]
  transfers between devices with their start and end apart: 2 -> 3, of which waited for: 1 -> 1; matrix products, arithmetic and copies ran while one was open for 2% -> 5% of each run, Pallas kernels for 0% -> 0%
where the time goes in v1:
time: 518 us; the launch traced here: 514 us
  blocking collectives  306 us (59%)
  matrix products  110 us (21%)
  waiting for transfers between devices  32 us (6%)
  other arithmetic  30.5 us (6%)
  between operations  18.9 us (4%)
  starting transfers between devices  9.15 us (2%)
  local copies, waits for them, and re-layouts  6.96 us (1%)
    psum x3, blocking collectives, on_device(): scale_cols = 1.0 / lax.psum(col_part, 'patch')  95.6 us
    psum x3, blocking collectives, on_device(): scale_rows = 1.0 / lax.psum(row_part, 'proto')  87.4 us
    psum x1, blocking collectives, on_device(): lax.psum((loss_partial, jnp.sum(row_weight.astype(jnp.float32))), ('patch...  73.2 us
    dot_general x3, matrix products, on_device(): row_part = jnp.dot(teacher_exp, scale_cols, precision=highest)  52.8 us
    psum x1, waiting for transfers between devices, on_device(): head_full = lax.psum(head_term(student_rows, grad_logits), 'patch')  32 us
    unnamed x1, blocking collectives  31.4 us
    dot_general x3, matrix products, on_device(): col_part = jnp.dot(scale_rows, teacher_exp, precision=highest)  30.8 us
    all_gather x1, blocking collectives, on_device(): lax.all_gather(own_student, 'proto', axis=0, tiled=True)  18.6 us
  transfers between devices with their start and end apart: 3, of which 1 were waited for; matrix products, arithmetic and copies ran while one was open for 5% of the time, Pallas kernels for 0%

profile of v1, /device:TPU:1, one launch (start us, length us, event | category | flops | bytes accessed | tf_op | source)
XLA Modules:
  0.0 514.1 jit_solution(8531392583103173211)
XLA Ops:
  8.0 0.7 compare_select_fusion
  8.7 0.7 compare_and_fusion
  10.0 1.5 gather_fusion.1
  11.8 0.7 stack.2
  12.6 8.6 %all-to-all-start = ((bf16[16,32,256]{2,1,0:T(8,128)(2,1)}), bf16[16,32,256]{2,1,0:T(8,128)(2,1)S(1)}, u32[]{:S(2)}, u32[]{:S(2)}) async-start(bf16[16,32,256]{2,1,0:T(8,128)(2,1)} %stack.2), calls=%async_computation | async-start | bytes 524288 | tf_op jit(solution)/shard_map/all_to_all | solution.py:57
  21.2 3.1 fusion
  24.3 18.6 %all_gather.7 = bf16[512,256]{1,0:T(8,128)(2,1)S(1)} all-gather(bf16[32,256]{1,0:T(8,128)(2,1)S(1)} %get-tuple-element.14), channel_id=1, replica_groups=mesh['patch'=8,'proto'=16] {'proto'}, dimensions={0}, use_global_device_ids=true | all-gather | bytes 278528 | tf_op jit(solution)/shard_map/all_gather | solution.py:59
  42.9 10.0 %exponential_reduce_fusion = (f32[512]{0:T(512)S(1)}, f32[512,8192]{1,0:T(8,128)}) fusion(bf16[512,256]{1,0:T(8,128)(2,1)S(1)} %all_gather.7, f32[8192]{0:T(1024)S(1)} %add_rsqrt_fusion, bf16[256,8192]{1,0:T(8,128)(2,1)} %param.9), kind=kOutput, calls=%fused_computation.6 | convolution fusion | flops 2162163200 | bytes 21268480 | tf_op jit(solution)/shard_map/dot_general | solution.py:72
  54.5 31.4 %all-reduce = bf16[512]{0:T(512)(128)(2,1)S(1)} all-reduce(bf16[512]{0:T(512)(128)(2,1)S(1)} %dynamic-update-slice), channel_id=1, replica_groups=mesh['patch'=8,'proto'=16] {'proto'}, use_global_device_ids=true, to_apply=%add | all-reduce | flops 512 | bytes 2048
  85.9 4.4 multiply_exponential_fusion
  90.4 7.9 %fusion.20 = f32[1,8192]{1,0:T(1,128)S(1)} fusion(f32[512,8192]{1,0:T(8,128)S(1)} %multiply_exponential_fusion), kind=kOutput, calls=%fused_computation.41 | convolution fusion | flops 50331648 | bytes 16809984 | tf_op jit(solution)/shard_map/dot_general | solution.py:68
  98.3 33.9 %psum.71 = f32[8192]{0:T(1024)S(1)} all-reduce(f32[8192]{0:T(1024)S(1)} %bitcast.35), channel_id=1, replica_groups=mesh['patch'=8,'proto'=16] {'patch'}, use_global_device_ids=true, to_apply=%region_5.7 | all-reduce | flops 8192 | bytes 65536 | tf_op jit(solution)/shard_map/psum | solution.py:69
  132.2 17.6 %fusion.23 = f32[1,512]{1,0:T(1,128)S(1)} fusion(f32[512,8192]{1,0:T(8,128)} %copy-done.2, f32[8192,1]{0,1:T(1,128)S(1)} %bitcast.31), kind=kOutput, calls=%fused_computation.50 | convolution fusion | flops 50331648 | bytes 16812032 | tf_op jit(solution)/shard_map/dot_general | solution.py:70
  149.9 28.5 %psum.72 = f32[512]{0:T(512)S(1)} all-reduce(f32[512]{0:T(512)S(1)} %bitcast.37), channel_id=1, replica_groups=mesh['patch'=8,'proto'=16] {'proto'}, use_global_device_ids=true, to_apply=%region_6.8 | all-reduce | flops 512 | bytes 4096 | tf_op jit(solution)/shard_map/psum | solution.py:71
  178.4 11.5 %fusion.24 = f32[1,8192]{1,0:T(1,128)S(1)} fusion(f32[512,1]{0,1:T(1,128)S(1)} %bitcast.39, f32[512,8192]{1,0:T(8,128)} %copy-done.2), kind=kOutput, calls=%fused_computation.51 | convolution fusion | flops 50331648 | bytes 16812032 | tf_op jit(solution)/shard_map/dot_general | solution.py:68
  189.8 30.8 %psum.73 = f32[8192]{0:T(1024)S(1)} all-reduce(f32[8192]{0:T(1024)S(1)} %bitcast.32), channel_id=1, replica_groups=mesh['patch'=8,'proto'=16] {'patch'}, use_global_device_ids=true, to_apply=%region_7.9 | all-reduce | flops 8192 | bytes 65536 | tf_op jit(solution)/shard_map/psum | solution.py:69
  220.6 17.6 %fusion.25 = f32[1,512]{1,0:T(1,128)S(1)} fusion(f32[512,8192]{1,0:T(8,128)} %copy-done.2, f32[8192,1]{0,1:T(1,128)S(1)} %bitcast.33), kind=kOutput, calls=%fused_computation.52 | convolution fusion | flops 50331648 | bytes 16812032 | tf_op jit(solution)/shard_map/dot_general | solution.py:70
  238.2 30.4 %psum.74 = f32[512]{0:T(512)S(1)} all-reduce(f32[512]{0:T(512)S(1)} %bitcast.38), channel_id=1, replica_groups=mesh['patch'=8,'proto'=16] {'proto'}, use_global_device_ids=true, to_apply=%region_8.10 | all-reduce | flops 512 | bytes 4096 | tf_op jit(solution)/shard_map/psum | solution.py:71
  268.6 11.5 %fusion.26 = f32[1,8192]{1,0:T(1,128)S(1)} fusion(f32[512,1]{0,1:T(1,128)S(1)} %bitcast.40, f32[512,8192]{1,0:T(8,128)} %copy-done.2), kind=kOutput, calls=%fused_computation.53 | convolution fusion | flops 50331648 | bytes 16812032 | tf_op jit(solution)/shard_map/dot_general | solution.py:68
  280.0 30.9 %psum.75 = f32[8192]{0:T(1024)S(1)} all-reduce(f32[8192]{0:T(1024)S(1)} %bitcast.34), channel_id=1, replica_groups=mesh['patch'=8,'proto'=16] {'patch'}, use_global_device_ids=true, to_apply=%region_9.11 | all-reduce | flops 8192 | bytes 65536 | tf_op jit(solution)/shard_map/psum | solution.py:69
  311.0 17.6 %fusion.27 = f32[1,512]{1,0:T(1,128)S(1)} fusion(f32[512,8192]{1,0:T(8,128)} %copy-done.2, f32[8192,1]{0,1:T(1,128)S(1)} %bitcast.30), kind=kOutput, calls=%fused_computation.54 | convolution fusion | flops 50331648 | bytes 16812032 | tf_op jit(solution)/shard_map/dot_general | solution.py:70
  328.6 28.5 %all-reduce.2 = (f32[512]{0:T(512)S(1)}, f32[512]{0:T(512)S(1)}) all-reduce(f32[512]{0:T(512)S(1)} %bitcast.36, f32[512]{0:T(512)S(1)} %get-tuple-element.16), channel_id=1, replica_groups=mesh['patch'=8,'proto'=16] {'proto'}, use_global_device_ids=true, to_apply=%region_10.12 | all-reduce | flops 1024 | bytes 8192 | tf_op jit(solution)/shard_map/psum | solution.py:71
  357.1 14.4 %multiply_reduce_fusion = (f32[]{:T(128)}, bf16[512,8192]{1,0:T(8,128)(2,1)S(1)}) fusion(f32[512,8192]{1,0:T(8,128)} %copy-done.2, f32[512,8192]{1,0:T(8,128)} %get-tuple-element.17, f32[512]{0:T(512)S(1)} %log.3, f32[8192]{0:T(1024)S(1)} %broadcast_divide_fusion, f32[512]{0:T(512)S(1)} %broadcast_divide_fusion.5, f32[512]{0:T(512)S(1)} %convert_element_type.28, ...), kind=kLoop, calls=%fused_computation.2 | loop fusion | flops 46137344 | bytes 41984004 | tf_op jit(solution)/shard_map/reduce_sum | solution.py:23
  371.6 3.2 copy-done.4
  374.8 3.2 fusion.7
  378.5 9.0 %convolution_multiply_fusion = f32[256,8192]{1,0:T(8,128)} fusion(bf16[512,256]{1,0:T(8,128)(2,1)S(1)} %all_gather.7, bf16[512,8192]{1,0:T(8,128)(2,1)} %copy-done.4), kind=kOutput, calls=%fused_computation.7 | convolution fusion | flops 2149580800 | bytes 17039360 | tf_op jit(solution)/shard_map/dot_general | solution.py:38
  388.1 73.2 %all-reduce.1 = (f32[]{:T(128)}, f32[]{:T(128)}) all-reduce(f32[]{:T(128)} %get-tuple-element.10, f32[]{:T(128)} %convert_reduce_fusion), channel_id=1, replica_groups=mesh['patch'=8,'proto'=16] {'patch','proto'}, use_global_device_ids=true, to_apply=%region_16.18 | all-reduce | flops 2 | bytes 16 | tf_op jit(solution)/shard_map/psum | solution.py:87
  462.7 0.9 fusion.14
  463.6 1.5 fusion.16
  465.1 32.0 %all-reduce.5.cloned.1.call-done = f32[256,8192]{1,0:T(8,128)} async-done(((f32[256,8192]{1,0:T(8,128)}), f32[256,8192]{1,0:T(8,128)}) %all-reduce.5.cloned.1.call-update) | async-done | bytes 8388624 | tf_op jit(solution)/shard_map/psum | solution.py:83
  497.1 6.0 %multiply_reduce_fusion.1 = (f32[8192]{0:T(1024)S(1)}, f32[256,8192]{1,0:T(8,128)S(1)}) fusion(f32[256,8192]{1,0:T(8,128)} %all-reduce.5.cloned.1.call-done, f32[8192]{0:T(1024)S(1)} %add_rsqrt_fusion, bf16[256,8192]{1,0:T(8,128)(2,1)} %param.9), kind=kLoop, calls=%fused_computation.11 | loop fusion | flops 8380416 | bytes 21037056 | tf_op jit(solution)/shard_map/reduce_sum | solution.py:84
  503.1 2.3 fusion.10
  (37 shorter events, 3.1 us)
Async XLA Ops:
  8.0 1.4 copy-start
  12.6 73.3 %all-to-all-start = ((bf16[16,32,256]{2,1,0:T(8,128)(2,1)}), bf16[16,32,256]{2,1,0:T(8,128)(2,1)S(1)}, u32[]{:S(2)}, u32[]{:S(2)}) async-start(bf16[16,32,256]{2,1,0:T(8,128)(2,1)} %stack.2), calls=%async_computation | async-start | bytes 524288 | tf_op jit(solution)/shard_map/all_to_all | solution.py:57
  21.2 441.5 %reduce-scatter.2.cloned.1.call-start = ((), (), s32[]{:S(2)}) async-start(), calls=%async_computation.2 | async-start | bytes 557056 | tf_op jit(solution)/shard_map/reduce_scatter | solution.py:78
  42.9 10.1 %copy-start.6 = (u32[128]{0:T(128)S(1)}, u32[128]{0:T(128)}, u32[]{:S(2)}) copy-start(u32[128]{0:T(128)} %constant.44) | copy-start | bytes 1540
  42.9 11.3 %copy-start.5 = (bf16[32]{0:T(256)(128)(2,1)S(1)}, bf16[32]{0:T(256)(128)(2,1)}, u32[]{:S(2)}) copy-start(bf16[32]{0:T(256)(128)(2,1)} %param.11) | copy-start | bytes 196
  90.3 8.0 %copy-start.2 = (f32[512,8192]{1,0:T(8,128)}, f32[512,8192]{1,0:T(8,128)S(1)}, u32[]{:S(2)}) copy-start(f32[512,8192]{1,0:T(8,128)S(1)} %multiply_exponential_fusion) | copy-start | bytes 50331652
  357.1 17.7 %copy-start.3 = (bf16[256,8192]{1,0:T(8,128)(2,1)S(1)}, bf16[256,8192]{1,0:T(8,128)(2,1)}, u32[]{:S(2)}) copy-start(bf16[256,8192]{1,0:T(8,128)(2,1)} %param.9) | copy-start | bytes 12582916
  371.6 3.2 copy-start.4
  378.0 119.1 %all-reduce.5.cloned.1.call-start = ((), (), s32[]{:S(2)}) async-start(), calls=%async_computation.3 | async-start | bytes 16777216 | tf_op jit(solution)/shard_map/psum | solution.py:83
  463.6 41.8 %copy-start.1 = (bf16[256,256]{1,0:T(8,128)(2,1)S(1)}, bf16[256,256]{1,0:T(8,128)(2,1)}, u32[]{:S(2)}) copy-start(bf16[256,256]{1,0:T(8,128)(2,1)} %param.7) | copy-start | bytes 393220
Sparse Core Ops, SparseCore 0:
  378.1 75.9 reduce-scatter.1
Sparse Core Ops, SparseCore 1:
  387.6 109.5 all-reduce.4
